TPU v7x, 256 devices: a whole 4x4x8 slice. The times are simulated.
256 devices in a mesh: shot: 8 (over x, y_lo), domain: 32 (over z, y_hi, core).
Axes of the slice: x: 4, y: 4 (y_hi: 2, y_lo: 2; y = y_hi * 2 + y_lo), z: 8, core: 2. Of those that a mesh axis runs over, the one named last changes fastest.
Arguments:
- velsq: float32 [64, 256, 128], P('domain', 'shot'), may hold values from 0.04 to 0.12
- epsilon: float32 [64, 256, 128], P('domain', 'shot'), may hold values from 0 to 0.3
- delta: float32 [64, 256, 128], P('domain', 'shot'), may hold values from 0 to 0.15
- tilt: float32 [64, 256, 128], P('domain', 'shot'), may hold values from -1.2 to 1.2
- azimuth: float32 [64, 256, 128], P('domain', 'shot'), may hold values from -3.140625 to 3.140625
- forward_state: float32 [8, 4, 64, 256, 128], P('shot', None, 'domain'), may hold values from -6 to 6
- adjoint_state: float32 [8, 4, 64, 256, 128], P('shot', None, 'domain'), may hold values from -6 to 6
- wavelet: float32 [8, 2], P('shot'), may hold values from -60 to 60
- source: int32 [8], P('shot'), may hold values from 0 to 2097151
- receivers: int32 [8, 256], P('shot'), may hold values from 0 to 2097151
- observed: float32 [8, 2, 256], P('shot'), may hold values from -18 to 18
Outputs:
- gradients: float32 [5, 64, 256, 128], P(None, 'domain', 'shot')
Inputs may be any that keep to these rules, and one draw needn't show every extreme that they name: `source`: flat index x * 256 * 128 + y * 128 + z of a grid cell. `receivers`: flat index x * 256 * 128 + y * 128 + z of a grid cell; cells may repeat.
All inputs are finite; a program needn't handle non-finite values.
Results may differ from a plain program's by a relative error of at most 0.0001.
Values sent between devices are 32-bit elements; how exact they have to be, the bound alone decides.
A program may use at most 128 MiB of HBM per device.

v0:
```python
import jax
import jax.numpy as jnp
from jax import lax
from jax.sharding import PartitionSpec as P

STEPS = 2


def with_halo(block, sides, width):
    for axis, dim in sides:
        count = lax.axis_size(axis)
        forward = [(i, i + 1) for i in range(count - 1)]
        backward = [(target, source) for source, target in forward]
        low = lax.ppermute(
            lax.slice_in_dim(block, block.shape[dim] - width, None, axis=dim), axis, forward
        )
        high = lax.ppermute(lax.slice_in_dim(block, 0, width, axis=dim), axis, backward)
        block = jnp.concatenate([low, block, high], axis=dim)
    return block


def hessian(values):
    padded = jnp.pad(values, ((0, 0), (1, 1), (1, 1)))
    center = padded[1:-1, 1:-1, 1:-1]
    curve_xx = padded[2:, 1:-1, 1:-1] + padded[:-2, 1:-1, 1:-1] - 2.0 * center
    curve_yy = padded[1:-1, 2:, 1:-1] + padded[1:-1, :-2, 1:-1] - 2.0 * center
    curve_zz = padded[1:-1, 1:-1, 2:] + padded[1:-1, 1:-1, :-2] - 2.0 * center
    mixed_xy = 0.25 * (
        padded[2:, 2:, 1:-1]
        - padded[2:, :-2, 1:-1]
        - padded[:-2, 2:, 1:-1]
        + padded[:-2, :-2, 1:-1]
    )
    mixed_xz = 0.25 * (
        padded[2:, 1:-1, 2:]
        - padded[2:, 1:-1, :-2]
        - padded[:-2, 1:-1, 2:]
        + padded[:-2, 1:-1, :-2]
    )
    mixed_yz = 0.25 * (
        padded[1:-1, 2:, 2:]
        - padded[1:-1, 2:, :-2]
        - padded[1:-1, :-2, 2:]
        + padded[1:-1, :-2, :-2]
    )
    return jnp.stack([curve_xx, curve_yy, curve_zz, mixed_xy, mixed_xz, mixed_yz])


def tables(velsq, epsilon, delta, tilt, azimuth):
    sin_tilt = jnp.sin(tilt)
    cos_tilt = jnp.cos(tilt)
    sin_azim = jnp.sin(azimuth)
    cos_azim = jnp.cos(azimuth)
    axis_x = sin_tilt * cos_azim
    axis_y = sin_tilt * sin_azim
    turn_x = cos_tilt * cos_azim
    turn_y = cos_tilt * sin_azim
    turn_z = -sin_tilt
    spin_x = -sin_tilt * sin_azim
    spin_y = sin_tilt * cos_azim
    along = jnp.stack(
        [
            axis_x * axis_x,
            axis_y * axis_y,
            cos_tilt * cos_tilt,
            2.0 * axis_x * axis_y,
            2.0 * axis_x * cos_tilt,
            2.0 * axis_y * cos_tilt,
        ]
    )
    by_tilt = jnp.stack(
        [
            2.0 * turn_x * axis_x,
            2.0 * turn_y * axis_y,
            2.0 * turn_z * cos_tilt,
            2.0 * (turn_x * axis_y + turn_y * axis_x),
            2.0 * (turn_x * cos_tilt + turn_z * axis_x),
            2.0 * (turn_y * cos_tilt + turn_z * axis_y),
        ]
    )
    by_spin = jnp.stack(
        [
            2.0 * spin_x * axis_x,
            2.0 * spin_y * axis_y,
            jnp.zeros_like(cos_tilt),
            2.0 * (spin_x * axis_y + spin_y * axis_x),
            2.0 * spin_x * cos_tilt,
            2.0 * spin_y * cos_tilt,
        ]
    )
    return (velsq, 1.0 + 2.0 * epsilon, jnp.sqrt(1.0 + 2.0 * delta), along, by_tilt, by_spin)


def operate(pad_p, pad_q, table, full):
    speed_sq, stretch, root_d, along, by_tilt, by_spin = table
    hess_p = hessian(pad_p)
    hess_q = hessian(pad_q)
    laplace = hess_p[0] + hess_p[1] + hess_p[2]
    axial_p = jnp.sum(along * hess_p, axis=0)
    axial_q = jnp.sum(along * hess_q, axis=0)
    across = laplace - axial_p
    drive_p = stretch * across + root_d * axial_q
    drive_q = root_d * across + axial_q
    if full:
        image_terms = (
            across,
            axial_q,
            jnp.sum(by_tilt * hess_p, axis=0),
            jnp.sum(by_tilt * hess_q, axis=0),
            jnp.sum(by_spin * hess_p, axis=0),
            jnp.sum(by_spin * hess_q, axis=0),
        )
        return (drive_p, drive_q, image_terms)
    return (drive_p, drive_q, ())


def advance(pad_p, pad_q, prior_p, prior_q, table, full):
    drive_p, drive_q, image_terms = operate(pad_p, pad_q, table, full)
    speed_sq = table[0]
    next_p = 2.0 * pad_p[1:-1] - prior_p + speed_sq * drive_p
    next_q = 2.0 * pad_q[1:-1] - prior_q + speed_sq * drive_q
    return (next_p, next_q, image_terms)


def correlate(gradient, adjoint_p, adjoint_q, image_terms, table):
    speed_sq, stretch, root_d, along, by_tilt, by_spin = table
    across, axial_q, tilt_p, tilt_q, spin_p, spin_q = image_terms
    g_speed = (
        gradient[0]
        + adjoint_p * (stretch * across + root_d * axial_q)
        + adjoint_q * (root_d * across + axial_q)
    )
    g_eps = gradient[1] + 2.0 * speed_sq * adjoint_p * across
    g_delta = gradient[2] + speed_sq * (adjoint_p * axial_q + adjoint_q * across) / root_d
    g_tilt = gradient[3] + speed_sq * (
        adjoint_p * (root_d * tilt_q - stretch * tilt_p) + adjoint_q * (tilt_q - root_d * tilt_p)
    )
    g_spin = gradient[4] + speed_sq * (
        adjoint_p * (root_d * spin_q - stretch * spin_p) + adjoint_q * (spin_q - root_d * spin_p)
    )
    return (g_speed, g_eps, g_delta, g_tilt, g_spin)


def inject(values, start_row, target, amount):
    layout = values.shape
    plane_size = layout[1] * layout[2]
    offset = target - start_row * plane_size
    inside = (offset >= 0) & (offset < layout[0] * plane_size)
    clipped = jnp.where(inside, offset, 0)
    return values.reshape(-1).at[clipped].add(jnp.where(inside, amount, 0.0)).reshape(layout)


def sample_cells(values, start_row, target):
    layout = values.shape
    plane_size = layout[1] * layout[2]
    offset = target - start_row * plane_size
    inside = (offset >= 0) & (offset < layout[0] * plane_size)
    clipped = jnp.where(inside, offset, 0)
    return jnp.where(inside, values.reshape(-1)[clipped], 0.0)


def single_rim(field_p, field_q):
    padded = with_halo(jnp.stack([field_p, field_q]), (("domain", 1),), 1)
    return (padded[0], padded[1])


def shards(
    velsq,
    epsilon,
    delta,
    tilt,
    azimuth,
    forward_state,
    adjoint_state,
    wavelet,
    source,
    receivers,
    observed,
):
    gathered = (
        lax.all_gather(velsq, "shot", axis=1, tiled=True),
        lax.all_gather(epsilon, "shot", axis=1, tiled=True),
        lax.all_gather(delta, "shot", axis=1, tiled=True),
        lax.all_gather(tilt, "shot", axis=1, tiled=True),
        lax.all_gather(azimuth, "shot", axis=1, tiled=True),
    )
    row_count = gathered[0].shape[0]
    first_row = lax.axis_index("domain") * row_count
    inner = tables(gathered[0], gathered[1], gathered[2], gathered[3], gathered[4])
    full_terms = False
    full_terms = True
    source_cell = source[0]
    receiver_cells = receivers[0]
    older_p, field_p, older_q, field_q = (
        forward_state[0, 0],
        forward_state[0, 1],
        forward_state[0, 2],
        forward_state[0, 3],
    )
    saved = []
    traces = []
    for moment in range(STEPS):
        pad_p, pad_q = single_rim(field_p, field_q)
        next_p, next_q, image_terms = advance(pad_p, pad_q, older_p, older_q, inner, full_terms)
        next_p = inject(next_p, first_row, source_cell, wavelet[0, moment])
        next_q = inject(next_q, first_row, source_cell, wavelet[0, moment])
        saved.append(image_terms)
        traces.append(sample_cells(next_p, first_row, receiver_cells))
        older_p, field_p, older_q, field_q = (field_p, next_p, field_q, next_q)
    recorded = lax.psum(jnp.stack(traces), "domain")
    misfit = recorded - observed[0]
    gradient = tuple((jnp.zeros(field_p.shape, jnp.float32) for member in range(5)))
    before_p, adjoint_p, before_q, adjoint_q = (
        adjoint_state[0, 0],
        adjoint_state[0, 1],
        adjoint_state[0, 2],
        adjoint_state[0, 3],
    )
    for moment in range(STEPS):
        back_index = STEPS - 1 - moment
        gradient = correlate(gradient, adjoint_p, adjoint_q, saved[back_index], inner)
        pad_p, pad_q = single_rim(adjoint_p, adjoint_q)
        next_p, next_q, unused = advance(pad_p, pad_q, before_p, before_q, inner, False)
        next_p = inject(next_p, first_row, receiver_cells, misfit[back_index])
        before_p, adjoint_p, before_q, adjoint_q = (adjoint_p, next_p, adjoint_q, next_q)
    return lax.psum_scatter(jnp.stack(gradient), "shot", scatter_dimension=2, tiled=True)


def solution(mesh):
    placed = (
        P("domain", "shot", None),
        P("domain", "shot", None),
        P("domain", "shot", None),
        P("domain", "shot", None),
        P("domain", "shot", None),
        P("shot", None, "domain", None, None),
        P("shot", None, "domain", None, None),
        P("shot", None),
        P("shot"),
        P("shot", None),
        P("shot", None, None),
    )
    return jax.shard_map(
        shards,
        mesh=mesh,
        in_specs=placed,
        out_specs=P(None, "domain", "shot", None),
        check_vma=False,
    )
```

profile of v0, /device:TPU:16, one launch (start us, length us, event | category | flops | bytes accessed | tf_op | source)
XLA Modules:
  0.0 354.3 jit_solution(16403042310096619500)
XLA Ops:
  6.5 1.2 slice_bitcast_fusion.9
  8.5 1.9 collective-permute-start.4
  10.4 2.4 collective-permute-start.5
  12.9 0.8 fusion.2
  13.7 4.8 %collective-permute-start = (f32[2,1,256,128]{3,2,1,0:T(8,128)}, f32[2,1,256,128]{3,2,1,0:T(8,128)}, u32[]{:S(2)}, u32[]{:S(2)}) collective-permute-start(f32[2,1,256,128]{3,2,1,0:T(8,128)} %get-tuple-element.99), channel_id=1, source_target_pairs={{1,0},{2,1},{3,2},{4,3},{5,4},{6,5},{7,6},{8,7},{9,8},{10,9},{11,1... | collective-permute-start | bytes 786440 | tf_op jit(solution)/shard_map/ppermute | solution.py:17
  18.5 2.6 collective-permute-start.1
  21.2 28.5 %all_gather.17 = f32[2,256,128]{2,1,0:T(8,128)S(1)} all-gather(f32[2,32,128]{2,1,0:T(8,128)S(1)} %copy-done.35), channel_id=1, replica_groups=mesh['shot'=8,'domain'=32] {'shot'}, dimensions={1}, use_global_device_ids=true | all-gather | bytes 294912 | tf_op jit(solution)/shard_map/all_gather | solution.py:184
  49.7 0.9 fusion.194
  50.6 28.6 %all_gather.18 = f32[2,256,128]{2,1,0:T(8,128)S(1)} all-gather(f32[2,32,128]{2,1,0:T(8,128)S(1)} %copy-done.36), channel_id=1, replica_groups=mesh['shot'=8,'domain'=32] {'shot'}, dimensions={1}, use_global_device_ids=true | all-gather | bytes 294912 | tf_op jit(solution)/shard_map/all_gather | solution.py:185
  79.2 0.9 fusion.193
  80.2 28.4 %all_gather.16 = f32[2,256,128]{2,1,0:T(8,128)S(1)} all-gather(f32[2,32,128]{2,1,0:T(8,128)S(1)} %copy-done.37), channel_id=1, replica_groups=mesh['shot'=8,'domain'=32] {'shot'}, dimensions={1}, use_global_device_ids=true | all-gather | bytes 294912 | tf_op jit(solution)/shard_map/all_gather | solution.py:181
  108.6 28.4 %all_gather.19 = f32[2,256,128]{2,1,0:T(8,128)S(1)} all-gather(f32[2,32,128]{2,1,0:T(8,128)S(1)} %copy-done.38), channel_id=1, replica_groups=mesh['shot'=8,'domain'=32] {'shot'}, dimensions={1}, use_global_device_ids=true | all-gather | bytes 294912 | tf_op jit(solution)/shard_map/all_gather | solution.py:183
  137.0 28.4 %all_gather.15 = f32[2,256,128]{2,1,0:T(8,128)S(1)} all-gather(f32[2,32,128]{2,1,0:T(8,128)S(1)} %copy-done.39), channel_id=1, replica_groups=mesh['shot'=8,'domain'=32] {'shot'}, dimensions={1}, use_global_device_ids=true | all-gather | bytes 294912 | tf_op jit(solution)/shard_map/all_gather | solution.py:182
  166.8 0.9 bitcast_dynamic-update-slice_fusion.9
  167.7 0.9 bitcast_dynamic-update-slice_fusion.26
  168.6 1.0 bitcast_dynamic-update-slice_fusion.8
  169.5 0.9 bitcast_dynamic-update-slice_fusion.7
  170.5 0.9 bitcast_dynamic-update-slice_fusion.6
  171.4 1.0 bitcast_dynamic-update-slice_fusion.5
  175.1 1.1 pad_maximum_fusion.2
  176.3 1.1 copy-done
  177.5 1.9 subtract_dynamic-update-slice_fusion
  179.5 0.9 bitcast_dynamic-update-slice_fusion.14
  180.4 0.9 fusion.108
  182.0 1.5 pad_maximum_fusion
  183.6 1.1 fusion.155
  184.9 1.1 fusion.28
  188.0 2.4 multiply_reduce_fusion.13
  190.4 1.4 fusion.177
  194.7 1.9 collective-permute-start.2
  196.6 2.6 collective-permute-start.3
  200.0 1.7 gather_fusion
  201.8 1.1 fusion.140
  202.8 1.0 fusion.146
  203.9 4.4 %collective-permute-done.3 = f32[2,1,256,128]{3,2,1,0:T(8,128)} collective-permute-done((f32[2,1,256,128]{3,2,1,0:T(8,128)}, f32[2,1,256,128]{3,2,1,0:T(8,128)}, u32[]{:S(2)}, u32[]{:S(2)}) %collective-permute-start.3) | collective-permute-done | bytes 262176 | tf_op jit(solution)/shard_map/ppermute | solution.py:14
  208.3 1.1 pad_maximum_fusion.1
  209.5 1.2 fusion.152
  213.8 5.6 %multiply_reduce_fusion.2 = (f32[2,256,128]{2,1,0:T(8,128)}, f32[2,256,128]{2,1,0:T(8,128)}, f32[2,256,128]{2,1,0:T(8,128)}, f32[2,256,128]{2,1,0:T(8,128)}, f32...) fusion(f32[6,2,256,128]{3,2,1,0:T(8,128)} %bitcast_dynamic-upda, ...), kind=kLoop, calls=%fused_computation.101 | loop fusion | flops 8650752 | bytes 17301504 | tf_op jit(solution)/shard_map/reduce_sum | solution.py:110
  219.4 2.2 fusion.182
  221.8 1.7 gather_fusion.1
  223.5 64.4 %psum.7 = f32[2,256]{1,0:T(2,128)S(1)} all-reduce(f32[2,256]{1,0:T(2,128)S(1)} %pad_maximum_fusion.18), channel_id=1, replica_groups=mesh['shot'=8,'domain'=32] {'domain'}, use_global_device_ids=true, to_apply=%region_6.7 | all-reduce | flops 512 | bytes 4096 | tf_op jit(solution)/shard_map/psum | solution.py:210
  287.9 2.1 fusion.160
  290.0 2.4 scatter_fusion
  292.5 2.0 bitcast_dynamic-update-slice_fusion.13
  295.3 0.9 bitcast_dynamic-update-slice_fusion.11
  296.6 1.0 bitcast_dynamic-update-slice_fusion.4
  297.8 1.0 bitcast_dynamic-update-slice_fusion
  298.8 48.7 %reduce-scatter.2.cloned.1.call-done = f32[5,2,32,128]{3,2,1,0:T(8,128)} async-done(((f32[5,2,256,128]{3,2,1,0:T(8,128)}), f32[5,2,32,128]{3,2,1,0:T(8,128)}) %reduce-scatter.2.cloned.1.call-update) | async-done | bytes 163856 | tf_op jit(solution)/shard_map/reduce_scatter | solution.py:226
  (134 shorter events, 14.6 us)
Async XLA Ops:
  6.5 6.3 %copy-start.1 = (f32[1,4,2,256,128]{4,3,2,1,0:T(8,128)S(1)}, f32[1,4,2,256,128]{4,3,2,1,0:T(8,128)}, u32[]{:S(2)}) copy-start(f32[1,4,2,256,128]{4,3,2,1,0:T(8,128)} %param.22) | copy-start | bytes 3145732
  6.5 340.9 %reduce-scatter.2.cloned.1.call-start = ((), (), s32[]{:S(2)}) async-start(), calls=%async_computation.1 | async-start | bytes 1474560 | tf_op jit(solution)/shard_map/reduce_scatter | solution.py:226
  7.7 167.3 %copy-start.11 = (f32[1,2,256,128]{3,2,1,0:T(8,128)}, f32[1,2,256,128]{3,2,1,0:T(8,128)S(1)}, u32[]{:S(2)}) copy-start(f32[1,2,256,128]{3,2,1,0:T(8,128)S(1)} %get-tuple-element.73) | copy-start | bytes 786436
  7.7 167.3 %copy-start.14 = (f32[1,2,256,128]{3,2,1,0:T(8,128)}, f32[1,2,256,128]{3,2,1,0:T(8,128)S(1)}, u32[]{:S(2)}) copy-start(f32[1,2,256,128]{3,2,1,0:T(8,128)S(1)} %get-tuple-element.74) | copy-start | bytes 786436
  7.7 13.5 %copy-start.35 = (f32[2,32,128]{2,1,0:T(8,128)S(1)}, f32[2,32,128]{2,1,0:T(8,128)}, u32[]{:S(2)}) copy-start(f32[2,32,128]{2,1,0:T(8,128)} %param.20) | copy-start | bytes 98308
  8.5 166.6 %collective-permute-start.4 = (f32[2,1,256,128]{3,2,1,0:T(8,128)}, f32[2,1,256,128]{3,2,1,0:T(8,128)}, u32[]{:S(2)}, u32[]{:S(2)}) collective-permute-start(f32[2,1,256,128]{3,2,1,0:T(8,128)} %get-tuple-element.91), channel_id=1, source_target_pairs={{1,0},{2,1},{3,2},{4,3},{5,4},{6,5},{7,6},{8,7},{9,8},{10,9},{11,1... | collective-permute-start | bytes 786440 | tf_op jit(solution)/shard_map/ppermute | solution.py:17
  10.4 40.3 %copy-start.36 = (f32[2,32,128]{2,1,0:T(8,128)S(1)}, f32[2,32,128]{2,1,0:T(8,128)}, u32[]{:S(2)}) copy-start(f32[2,32,128]{2,1,0:T(8,128)} %param.21) | copy-start | bytes 98308
  10.4 164.7 %collective-permute-start.5 = (f32[2,1,256,128]{3,2,1,0:T(8,128)S(1)}, f32[2,1,256,128]{3,2,1,0:T(8,128)}, u32[]{:S(2)}, u32[]{:S(2)}) collective-permute-start(f32[2,1,256,128]{3,2,1,0:T(8,128)S(1)} %get-tuple-element.92), channel_id=1, source_target_pairs={{0,1},{1,2},{2,3},{3,4},{4,5},{5,6},{6,7},{7,8},{8,9},{9,10},{10,1... | collective-permute-start | bytes 786440 | tf_op jit(solution)/shard_map/ppermute | solution.py:14
  12.9 67.3 %copy-start.5 = (f32[1,2,256,128]{3,2,1,0:T(8,128)}, f32[1,2,256,128]{3,2,1,0:T(8,128)S(1)}, u32[]{:S(2)}) copy-start(f32[1,2,256,128]{3,2,1,0:T(8,128)S(1)} %get-tuple-element.86) | copy-start | bytes 786436
  12.9 171.9 %copy-start.3 = (f32[1,2,256,128]{3,2,1,0:T(8,128)}, f32[1,2,256,128]{3,2,1,0:T(8,128)S(1)}, u32[]{:S(2)}) copy-start(f32[1,2,256,128]{3,2,1,0:T(8,128)S(1)} %get-tuple-element.85) | copy-start | bytes 786436
  12.9 67.3 %copy-start.37 = (f32[2,32,128]{2,1,0:T(8,128)S(1)}, f32[2,32,128]{2,1,0:T(8,128)}, u32[]{:S(2)}) copy-start(f32[2,32,128]{2,1,0:T(8,128)} %param.17) | copy-start | bytes 98308
  12.9 95.7 %copy-start.38 = (f32[2,32,128]{2,1,0:T(8,128)S(1)}, f32[2,32,128]{2,1,0:T(8,128)}, u32[]{:S(2)}) copy-start(f32[2,32,128]{2,1,0:T(8,128)} %param.19) | copy-start | bytes 98308
  13.7 123.3 %copy-start.39 = (f32[2,32,128]{2,1,0:T(8,128)S(1)}, f32[2,32,128]{2,1,0:T(8,128)}, u32[]{:S(2)}) copy-start(f32[2,32,128]{2,1,0:T(8,128)} %param.18) | copy-start | bytes 98308
  13.7 151.6 %copy-start.41 = (f32[1,2]{1,0:T(1,128)S(1)}, f32[1,2]{1,0:T(1,128)}, u32[]{:S(2)}) copy-start(f32[1,2]{1,0:T(1,128)} %param.24) | copy-start | bytes 28
  13.7 168.3 %collective-permute-start = (f32[2,1,256,128]{3,2,1,0:T(8,128)}, f32[2,1,256,128]{3,2,1,0:T(8,128)}, u32[]{:S(2)}, u32[]{:S(2)}) collective-permute-start(f32[2,1,256,128]{3,2,1,0:T(8,128)} %get-tuple-element.99), channel_id=1, source_target_pairs={{1,0},{2,1},{3,2},{4,3},{5,4},{6,5},{7,6},{8,7},{9,8},{10,9},{11,1... | collective-permute-start | bytes 786440 | tf_op jit(solution)/shard_map/ppermute | solution.py:17
  18.5 163.5 %collective-permute-start.1 = (f32[2,1,256,128]{3,2,1,0:T(8,128)}, f32[2,1,256,128]{3,2,1,0:T(8,128)}, u32[]{:S(2)}, u32[]{:S(2)}) collective-permute-start(f32[2,1,256,128]{3,2,1,0:T(8,128)} %get-tuple-element.100), channel_id=1, source_target_pairs={{0,1},{1,2},{2,3},{3,4},{4,5},{5,6},{6,7},{7,8},{8,9},{9,10},{10,1... | collective-permute-start | bytes 786440 | tf_op jit(solution)/shard_map/ppermute | solution.py:14
  169.5 1.8 copy-start.40
  176.2 1.2 copy-start
  176.2 1.3 copy-start.12
  176.2 1.3 copy-start.15
  180.4 1.6 copy-start.6
  182.0 1.6 copy-start.25
  183.5 1.4 copy-start.2
  187.3 3.1 copy-start.9
  188.0 2.4 copy-start.7
  188.0 2.4 copy-start.4
  190.4 1.4 copy-start.16
  191.8 2.1 copy-start.18
  194.7 9.2 %collective-permute-start.2 = (f32[2,1,256,128]{3,2,1,0:T(8,128)}, f32[2,1,256,128]{3,2,1,0:T(8,128)}, u32[]{:S(2)}, u32[]{:S(2)}) collective-permute-start(f32[2,1,256,128]{3,2,1,0:T(8,128)} %get-tuple-element.97), channel_id=1, source_target_pairs={{1,0},{2,1},{3,2},{4,3},{5,4},{6,5},{7,6},{8,7},{9,8},{10,9},{11,1... | collective-permute-start | bytes 786440 | tf_op jit(solution)/shard_map/ppermute | solution.py:17
  196.6 11.7 %collective-permute-start.3 = (f32[2,1,256,128]{3,2,1,0:T(8,128)}, f32[2,1,256,128]{3,2,1,0:T(8,128)}, u32[]{:S(2)}, u32[]{:S(2)}) collective-permute-start(f32[2,1,256,128]{3,2,1,0:T(8,128)} %get-tuple-element.98), channel_id=1, source_target_pairs={{0,1},{1,2},{2,3},{3,4},{4,5},{5,6},{6,7},{7,8},{8,9},{9,10},{10,1... | collective-permute-start | bytes 786440 | tf_op jit(solution)/shard_map/ppermute | solution.py:14
  209.4 1.2 copy-start.24
  210.7 1.0 copy-start.22
  211.4 1.4 copy-start.26
  211.8 1.6 copy-start.8
  211.8 2.0 copy-start.10
  219.4 2.2 copy-start.20
  219.4 68.5 %copy-start.42 = (f32[1,2,256]{2,1,0:T(2,128)S(1)}, f32[1,2,256]{2,1,0:T(2,128)}, u32[]{:S(2)}) copy-start(f32[1,2,256]{2,1,0:T(2,128)} %param.27) | copy-start | bytes 6148
  219.4 68.5 %copy-start.13 = (f32[1,2,256,128]{3,2,1,0:T(8,128)S(1)}, f32[1,2,256,128]{3,2,1,0:T(8,128)}, u32[]{:S(2)}) copy-start(f32[1,2,256,128]{3,2,1,0:T(8,128)} %copy-done.11) | copy-start | bytes 786436
  290.0 2.4 copy-start.17
  290.0 2.4 copy-start.19
  290.0 2.4 copy-start.21
  290.0 2.4 copy-start.23
  295.3 1.0 copy-start.32
  295.3 1.2 copy-start.33
  295.3 1.3 copy-start.34
  296.6 1.0 copy-start.28
  296.6 1.1 copy-start.29
  296.6 1.3 copy-start.30
  (2 other events, 1.9 us)
Sparse Core Ops, SparseCore 0:
  298.9 48.4 reduce-scatter.1
where the time goes:
time: 355 us; the launch traced here: 354 us
  blocking collectives  207 us (58%)
  waiting for transfers between devices  53.1 us (15%)
  other arithmetic  51.8 us (15%)
  starting transfers between devices  16.2 us (5%)
  between operations  16 us (5%)
  local copies, waits for them, and re-layouts  10.5 us (3%)
    psum x1, blocking collectives, shards(): recorded = lax.psum(jnp.stack(traces), 'domain')  64.4 us
    reduce_scatter x1, waiting for transfers between devices, shards(): lax.psum_scatter(jnp.stack(gradient), 'shot', scatter_dimension=2, tiled=...  48.7 us
    all_gather x1, blocking collectives, shards(): lax.all_gather(azimuth, 'shot', axis=1, tiled=True)  28.6 us
    all_gather x1, blocking collectives, shards(): lax.all_gather(tilt, 'shot', axis=1, tiled=True)  28.5 us
    all_gather x1, blocking collectives, shards(): lax.all_gather(velsq, 'shot', axis=1, tiled=True)  28.4 us
    all_gather x1, blocking collectives, shards(): lax.all_gather(delta, 'shot', axis=1, tiled=True)  28.4 us
    all_gather x1, blocking collectives, shards(): lax.all_gather(epsilon, 'shot', axis=1, tiled=True)  28.4 us
    unnamed x33, other arithmetic  22 us
  transfers between devices with their start and end apart: 7, of which 2 were waited for; matrix products, arithmetic and copies ran while one was open for 6% of the time, Pallas kernels for 0%

commit v1 on v0

--- a/solution.py
+++ b/solution.py
@@ -1,9 +1,24 @@
+import functools
 import jax
 import jax.numpy as jnp
 from jax import lax
 from jax.sharding import PartitionSpec as P
+from jax.lax import all_to_all, axis_size
 
 STEPS = 2
+
+
+def connect_copies_up(mine_x, mesh_name):
+    blocks_here = []
+    for _ in range(axis_size(mesh_name)):
+        blocks_here.append(mine_x)
+    current_value = jnp.concatenate(
+        all_to_all(jnp.stack(blocks_here), split_axis=0, concat_axis=0, axis_name=mesh_name), axis=1
+    )
+    return current_value
+
+
+view_mark = functools.partial(connect_copies_up, mesh_name="shot")
 
 
 def with_halo(block, sides, width):
@@ -179,7 +194,7 @@
 ):
     gathered = (
         lax.all_gather(velsq, "shot", axis=1, tiled=True),
-        lax.all_gather(epsilon, "shot", axis=1, tiled=True),
+        view_mark(epsilon),
         lax.all_gather(delta, "shot", axis=1, tiled=True),
         lax.all_gather(tilt, "shot", axis=1, tiled=True),
         lax.all_gather(azimuth, "shot", axis=1, tiled=True),

time: 355 us -> 334 us (0.941)
  blocking collectives: 207 us -> 177 us
  local copies, waits for them, and re-layouts: 10.5 us -> 16.6 us
  starting transfers between devices: 16.2 us -> 21.4 us
  other arithmetic: 51.8 us -> 47 us
    all_gather x1 -> x0, blocking collectives: 28.4 us -> none  [shards(): lax.all_gather(epsilon, 'shot', axis=1, tiled=True)]
    unnamed x86 -> x90, local copies, waits for them, and re-layouts: 3.19 us -> 8.56 us
    all_to_all x0 -> x1, starting transfers between devices: none -> 5.02 us  [connect_copies_up(): all_to_all(jnp.stack(blocks_here), split_axis=0, concat_axis=0, axis_name...]
    unnamed x33 -> x32, other arithmetic: 22 us -> 17.8 us
  transfers between devices with their start and end apart: 7 -> 8, of which waited for: 2 -> 2; matrix products, arithmetic and copies ran while one was open for 6% -> 6% of each run, Pallas kernels for 0% -> 0%
where the time goes in v1:
time: 334 us; the launch traced here: 333 us
  blocking collectives  177 us (53%)
  waiting for transfers between devices  55.2 us (17%)
  other arithmetic  47 us (14%)
  starting transfers between devices  21.4 us (6%)
  local copies, waits for them, and re-layouts  16.6 us (5%)
  between operations  16 us (5%)
    psum x1, blocking collectives, shards(): recorded = lax.psum(jnp.stack(traces), 'domain')  62.9 us
    reduce_scatter x1, waiting for transfers between devices, shards(): lax.psum_scatter(jnp.stack(gradient), 'shot', scatter_dimension=2, tiled=...  50.4 us
    all_gather x1, blocking collectives, shards(): lax.all_gather(tilt, 'shot', axis=1, tiled=True)  29 us
    all_gather x1, blocking collectives, shards(): lax.all_gather(azimuth, 'shot', axis=1, tiled=True)  28.5 us
    all_gather x1, blocking collectives, shards(): lax.all_gather(delta, 'shot', axis=1, tiled=True)  28.4 us
    all_gather x1, blocking collectives, shards(): lax.all_gather(velsq, 'shot', axis=1, tiled=True)  28.4 us
    unnamed x32, other arithmetic  17.8 us
    ppermute x3, starting transfers between devices, with_halo(): lax.ppermute(lax.slice_in_dim(block, 0, width, axis=dim), axis, backward)  8.73 us
  transfers between devices with their start and end apart: 8, of which 2 were waited for; matrix products, arithmetic and copies ran while one was open for 6% of the time, Pallas kernels for 0%

profile of v1, /device:TPU:16, one launch (start us, length us, event | category | flops | bytes accessed | tf_op | source)
XLA Modules:
  0.0 333.5 jit_solution(17520840737026751404)
XLA Ops:
  6.5 1.2 slice_bitcast_fusion.9
  7.7 0.8 fusion
  8.6 2.0 collective-permute-start.4
  10.6 2.4 collective-permute-start.5
  13.1 0.8 fusion.2
  13.9 4.8 %collective-permute-start = (f32[2,1,256,128]{3,2,1,0:T(8,128)}, f32[2,1,256,128]{3,2,1,0:T(8,128)}, u32[]{:S(2)}, u32[]{:S(2)}) collective-permute-start(f32[2,1,256,128]{3,2,1,0:T(8,128)} %get-tuple-element.108), channel_id=1, source_target_pairs={{1,0},{2,1},{3,2},{4,3},{5,4},{6,5},{7,6},{8,7},{9,8},{10,9},{11,1... | collective-permute-start | bytes 786440 | tf_op jit(solution)/shard_map/ppermute | solution.py:32
  18.7 2.6 collective-permute-start.1
  22.1 5.0 %all-to-all-start = ((f32[8,2,32,128]{3,2,1,0:T(8,128)}), f32[8,2,32,128]{3,2,1,0:T(8,128)}, u32[]{:S(2)}, u32[]{:S(2)}) async-start(f32[8,2,32,128]{3,2,1,0:T(8,128)} %stack.213), calls=%async_computation | async-start | bytes 524288 | tf_op jit(solution)/shard_map/all_to_all | solution.py:16
  27.2 29.0 %all_gather.13 = f32[2,256,128]{2,1,0:T(8,128)S(1)} all-gather(f32[2,32,128]{2,1,0:T(8,128)S(1)} %copy-done.38), channel_id=1, replica_groups=mesh['shot'=8,'domain'=32] {'shot'}, dimensions={1}, use_global_device_ids=true | all-gather | bytes 294912 | tf_op jit(solution)/shard_map/all_gather | solution.py:199
  56.2 0.9 fusion.211
  57.2 28.5 %all_gather.14 = f32[2,256,128]{2,1,0:T(8,128)S(1)} all-gather(f32[2,32,128]{2,1,0:T(8,128)S(1)} %copy-done.39), channel_id=1, replica_groups=mesh['shot'=8,'domain'=32] {'shot'}, dimensions={1}, use_global_device_ids=true | all-gather | bytes 294912 | tf_op jit(solution)/shard_map/all_gather | solution.py:200
  85.7 0.9 fusion.210
  86.7 28.4 %all_gather.12 = f32[2,256,128]{2,1,0:T(8,128)S(1)} all-gather(f32[2,32,128]{2,1,0:T(8,128)S(1)} %copy-done.40), channel_id=1, replica_groups=mesh['shot'=8,'domain'=32] {'shot'}, dimensions={1}, use_global_device_ids=true | all-gather | bytes 294912 | tf_op jit(solution)/shard_map/all_gather | solution.py:196
  117.5 0.8 bitcast_dynamic-update-slice_fusion.7
  119.2 1.2 copy-done.3
  120.4 1.1 copy-done.28
  122.9 28.4 %all_gather.15 = f32[2,256,128]{2,1,0:T(8,128)S(1)} all-gather(f32[2,32,128]{2,1,0:T(8,128)S(1)} %copy-done.41), channel_id=1, replica_groups=mesh['shot'=8,'domain'=32] {'shot'}, dimensions={1}, use_global_device_ids=true | all-gather | bytes 294912 | tf_op jit(solution)/shard_map/all_gather | solution.py:198
  153.2 1.0 fusion.199
  155.8 1.1 copy-done
  157.8 0.8 fusion.124
  158.6 1.0 fusion.128
  159.6 0.9 fusion.108
  160.6 1.2 fusion.140
  161.8 1.1 pad_maximum_fusion
  163.0 1.1 copy-done.2
  164.1 1.2 subtract_dynamic-update-slice_fusion.2
  168.6 2.0 fusion.195
  172.8 1.9 collective-permute-start.2
  174.7 2.6 collective-permute-start.3
  177.3 1.0 fusion.146
  178.3 1.7 gather_fusion
  180.0 1.0 fusion.114
  181.1 1.1 fusion.120
  182.2 4.8 %collective-permute-done.3 = f32[2,1,256,128]{3,2,1,0:T(8,128)} collective-permute-done((f32[2,1,256,128]{3,2,1,0:T(8,128)}, f32[2,1,256,128]{3,2,1,0:T(8,128)}, u32[]{:S(2)}, u32[]{:S(2)}) %collective-permute-start.3) | collective-permute-done | bytes 262176 | tf_op jit(solution)/shard_map/ppermute | solution.py:29
  186.9 1.1 pad_maximum_fusion.1
  188.1 1.2 subtract_dynamic-update-slice_fusion.1
  192.8 5.1 %multiply_reduce_fusion.3 = (f32[2,256,128]{2,1,0:T(8,128)}, f32[2,256,128]{2,1,0:T(8,128)}, f32[2,256,128]{2,1,0:T(8,128)}, f32[2,256,128]{2,1,0:T(8,128)}, f32...) fusion(f32[6,2,256,128]{3,2,1,0:T(8,128)} %bitcast_dynamic-upda, ...), kind=kLoop, calls=%fused_computation.102 | loop fusion | flops 8650752 | bytes 17301504 | tf_op jit(solution)/shard_map/reduce_sum | solution.py:126
  197.9 2.3 fusion.196
  200.3 1.7 gather_fusion.1
  202.1 62.9 %psum.7 = f32[2,256]{1,0:T(2,128)S(1)} all-reduce(f32[2,256]{1,0:T(2,128)S(1)} %pad_maximum_fusion.18), channel_id=1, replica_groups=mesh['shot'=8,'domain'=32] {'domain'}, use_global_device_ids=true, to_apply=%region_6.7 | all-reduce | flops 512 | bytes 4096 | tf_op jit(solution)/shard_map/psum | solution.py:225
  265.0 2.5 fusion.160
  267.5 2.4 scatter_fusion
  270.0 1.5 fusion.194
  271.5 0.9 bitcast_dynamic-update-slice_fusion.13
  273.3 0.9 bitcast_dynamic-update-slice_fusion.11
  274.3 0.9 bitcast_dynamic-update-slice_fusion.4
  275.4 0.8 bitcast_dynamic-update-slice_fusion
  276.2 50.4 %reduce-scatter.2.cloned.1.call-done = f32[5,2,32,128]{3,2,1,0:T(8,128)} async-done(((f32[5,2,256,128]{3,2,1,0:T(8,128)}), f32[5,2,32,128]{3,2,1,0:T(8,128)}) %reduce-scatter.2.cloned.1.call-update) | async-done | bytes 163856 | tf_op jit(solution)/shard_map/reduce_scatter | solution.py:241
  (141 shorter events, 18.1 us)
Async XLA Ops:
  6.5 6.5 %copy-start.1 = (f32[1,4,2,256,128]{4,3,2,1,0:T(8,128)S(1)}, f32[1,4,2,256,128]{4,3,2,1,0:T(8,128)}, u32[]{:S(2)}) copy-start(f32[1,4,2,256,128]{4,3,2,1,0:T(8,128)} %param.22) | copy-start | bytes 3145732
  7.7 148.1 %copy-start.12 = (f32[1,2,256,128]{3,2,1,0:T(8,128)}, f32[1,2,256,128]{3,2,1,0:T(8,128)S(1)}, u32[]{:S(2)}) copy-start(f32[1,2,256,128]{3,2,1,0:T(8,128)S(1)} %get-tuple-element.79) | copy-start | bytes 786436
  7.7 148.1 %copy-start.13 = (f32[1,2,256,128]{3,2,1,0:T(8,128)}, f32[1,2,256,128]{3,2,1,0:T(8,128)S(1)}, u32[]{:S(2)}) copy-start(f32[1,2,256,128]{3,2,1,0:T(8,128)S(1)} %get-tuple-element.80) | copy-start | bytes 786436
  7.7 13.7 %copy-start.37 = (f32[2,32,128]{2,1,0:T(8,128)S(1)}, f32[2,32,128]{2,1,0:T(8,128)}, u32[]{:S(2)}) copy-start(f32[2,32,128]{2,1,0:T(8,128)} %param.18) | copy-start | bytes 98308
  8.6 18.6 %copy-start.38 = (f32[2,32,128]{2,1,0:T(8,128)S(1)}, f32[2,32,128]{2,1,0:T(8,128)}, u32[]{:S(2)}) copy-start(f32[2,32,128]{2,1,0:T(8,128)} %param.20) | copy-start | bytes 98308
  8.6 145.6 %collective-permute-start.4 = (f32[2,1,256,128]{3,2,1,0:T(8,128)}, f32[2,1,256,128]{3,2,1,0:T(8,128)S(1)}, u32[]{:S(2)}, u32[]{:S(2)}) collective-permute-start(f32[2,1,256,128]{3,2,1,0:T(8,128)} %get-tuple-element.99), channel_id=1, source_target_pairs={{1,0},{2,1},{3,2},{4,3},{5,4},{6,5},{7,6},{8,7},{9,8},{10,9},{11,1... | collective-permute-start | bytes 786440 | tf_op jit(solution)/shard_map/ppermute | solution.py:32
  10.6 143.6 %collective-permute-start.5 = (f32[2,1,256,128]{3,2,1,0:T(8,128)}, f32[2,1,256,128]{3,2,1,0:T(8,128)S(1)}, u32[]{:S(2)}, u32[]{:S(2)}) collective-permute-start(f32[2,1,256,128]{3,2,1,0:T(8,128)} %get-tuple-element.100), channel_id=1, source_target_pairs={{0,1},{1,2},{2,3},{3,4},{4,5},{5,6},{6,7},{7,8},{8,9},{9,10},{10,1... | collective-permute-start | bytes 786440 | tf_op jit(solution)/shard_map/ppermute | solution.py:29
  13.1 44.1 %copy-start.39 = (f32[2,32,128]{2,1,0:T(8,128)S(1)}, f32[2,32,128]{2,1,0:T(8,128)}, u32[]{:S(2)}) copy-start(f32[2,32,128]{2,1,0:T(8,128)} %param.21) | copy-start | bytes 98308
  13.9 72.8 %copy-start.40 = (f32[2,32,128]{2,1,0:T(8,128)S(1)}, f32[2,32,128]{2,1,0:T(8,128)}, u32[]{:S(2)}) copy-start(f32[2,32,128]{2,1,0:T(8,128)} %param.17) | copy-start | bytes 98308
  13.9 147.9 %collective-permute-start = (f32[2,1,256,128]{3,2,1,0:T(8,128)}, f32[2,1,256,128]{3,2,1,0:T(8,128)}, u32[]{:S(2)}, u32[]{:S(2)}) collective-permute-start(f32[2,1,256,128]{3,2,1,0:T(8,128)} %get-tuple-element.108), channel_id=1, source_target_pairs={{1,0},{2,1},{3,2},{4,3},{5,4},{6,5},{7,6},{8,7},{9,8},{10,9},{11,1... | collective-permute-start | bytes 786440 | tf_op jit(solution)/shard_map/ppermute | solution.py:32
  18.7 143.1 %collective-permute-start.1 = (f32[2,1,256,128]{3,2,1,0:T(8,128)}, f32[2,1,256,128]{3,2,1,0:T(8,128)}, u32[]{:S(2)}, u32[]{:S(2)}) collective-permute-start(f32[2,1,256,128]{3,2,1,0:T(8,128)} %get-tuple-element.109), channel_id=1, source_target_pairs={{0,1},{1,2},{2,3},{3,4},{4,5},{5,6},{6,7},{7,8},{8,9},{9,10},{10,1... | collective-permute-start | bytes 786440 | tf_op jit(solution)/shard_map/ppermute | solution.py:29
  22.1 131.1 %all-to-all-start = ((f32[8,2,32,128]{3,2,1,0:T(8,128)}), f32[8,2,32,128]{3,2,1,0:T(8,128)}, u32[]{:S(2)}, u32[]{:S(2)}) async-start(f32[8,2,32,128]{3,2,1,0:T(8,128)} %stack.213), calls=%async_computation | async-start | bytes 524288 | tf_op jit(solution)/shard_map/all_to_all | solution.py:16
  27.1 299.5 %reduce-scatter.2.cloned.1.call-start = ((), (), s32[]{:S(2)}) async-start(), calls=%async_computation.2 | async-start | bytes 1474560 | tf_op jit(solution)/shard_map/reduce_scatter | solution.py:241
  118.4 3.9 %copy-start.42 = (s32[1,256]{1,0:T(1,128)S(1)}, s32[1,256]{1,0:T(1,128)}, u32[]{:S(2)}) copy-start(s32[1,256]{1,0:T(1,128)} %param.26) | copy-start | bytes 3076
  118.4 3.9 %copy-start.43 = (f32[1,2]{1,0:T(1,128)S(1)}, f32[1,2]{1,0:T(1,128)}, u32[]{:S(2)}) copy-start(f32[1,2]{1,0:T(1,128)} %param.24) | copy-start | bytes 28
  118.4 4.5 %copy-start.41 = (f32[2,32,128]{2,1,0:T(8,128)S(1)}, f32[2,32,128]{2,1,0:T(8,128)}, u32[]{:S(2)}) copy-start(f32[2,32,128]{2,1,0:T(8,128)} %param.19) | copy-start | bytes 98308
  119.2 1.2 copy-start.3
  120.4 1.1 copy-start.28
  155.7 1.2 copy-start
  155.7 1.3 copy-start.24
  155.7 1.3 copy-start.26
  160.6 2.4 copy-start.30
  162.9 1.2 copy-start.2
  166.0 1.4 copy-start.4
  166.7 1.2 copy-start.6
  167.4 1.2 copy-start.8
  170.6 2.2 copy-start.10
  171.2 18.2 %copy-start.16 = (f32[65536]{0:T(1024)}, f32[65536]{0:T(1024)S(1)}, u32[]{:S(2)}) copy-start(f32[65536]{0:T(1024)S(1)} %broadcast_multiply_fusion.1) | copy-start | bytes 786436
  172.8 9.4 %collective-permute-start.2 = (f32[2,1,256,128]{3,2,1,0:T(8,128)}, f32[2,1,256,128]{3,2,1,0:T(8,128)}, u32[]{:S(2)}, u32[]{:S(2)}) collective-permute-start(f32[2,1,256,128]{3,2,1,0:T(8,128)} %get-tuple-element.105), channel_id=1, source_target_pairs={{1,0},{2,1},{3,2},{4,3},{5,4},{6,5},{7,6},{8,7},{9,8},{10,9},{11,1... | collective-permute-start | bytes 786440 | tf_op jit(solution)/shard_map/ppermute | solution.py:32
  174.7 12.3 %collective-permute-start.3 = (f32[2,1,256,128]{3,2,1,0:T(8,128)}, f32[2,1,256,128]{3,2,1,0:T(8,128)}, u32[]{:S(2)}, u32[]{:S(2)}) collective-permute-start(f32[2,1,256,128]{3,2,1,0:T(8,128)} %get-tuple-element.106), channel_id=1, source_target_pairs={{0,1},{1,2},{2,3},{3,4},{4,5},{5,6},{6,7},{7,8},{8,9},{9,10},{10,1... | collective-permute-start | bytes 786440 | tf_op jit(solution)/shard_map/ppermute | solution.py:29
  189.3 2.2 copy-start.31
  189.4 1.1 copy-start.27
  189.6 1.9 copy-start.29
  190.1 1.8 copy-start.9
  190.5 1.9 copy-start.5
  190.5 2.3 copy-start.7
  192.8 5.1 %copy-start.17 = (f32[65536]{0:T(1024)S(1)}, f32[65536]{0:T(1024)}, u32[]{:S(2)}) copy-start(f32[65536]{0:T(1024)} %copy-done.16) | copy-start | bytes 786436
  197.9 2.3 copy-start.14
  197.9 67.1 %copy-start.44 = (f32[1,2,256]{2,1,0:T(2,128)S(1)}, f32[1,2,256]{2,1,0:T(2,128)}, u32[]{:S(2)}) copy-start(f32[1,2,256]{2,1,0:T(2,128)} %param.27) | copy-start | bytes 6148
  267.5 2.4 copy-start.19
  267.5 2.4 copy-start.20
  269.9 1.6 copy-start.11
  269.9 1.6 copy-start.15
  269.9 1.6 copy-start.18
  269.9 1.6 copy-start.34
  269.9 1.6 copy-start.35
  273.3 1.0 copy-start.33
  274.3 1.1 copy-start.36
  (5 other events, 4.3 us)
Sparse Core Ops, SparseCore 0:
  276.4 50.2 reduce-scatter.1
